TPU v7x, 32 devices: a whole 2x2x4 slice. The times are simulated.
32 devices in a mesh: group: 2 (over y), chan: 4 (over z), band: 2 (over x), beam: 2 (over core).
Axes of the slice: x: 2, y: 2, z: 4, core: 2. Of those that a mesh axis runs over, the one named last changes fastest.
Arguments:
- voltages: bfloat16 [2, 1024, 2, 8, 512], P(None, 'chan', 'band', None, 'group'), parts along dimension 4, may hold values from -6 to 6
- gains: float32 [2, 2, 8, 1024], P(None, 'band', 'chan'), may hold values from -5 to 5
- positions: float32 [3, 1024], replicated, may hold values from -4 to 4
- directions: float32 [3, 2048], P(None, ('group', 'beam')), parts along dimension 1, may hold values from -1 to 1
- antenna_row_lookup: int32 [1024], replicated, may hold values from 0 to 1023, each once
- chan_order: int32 [16], replicated, may hold values from 0 to 15, each once
- delays: int32 [4, 2, 8], replicated, may hold values from 0 to 31
Outputs:
- dedispersed: float32 [2, 8, 32, 2048], P('band', 'chan', None, ('group', 'beam')), parts along dimension 3
There are 2 independent parts, one for each index of `group`. A program takes and returns all parts, laid end to end along the dimension named above; an argument that names none is the same for every part. Nothing has to cross between parts.
Inputs may be any that keep to these rules, and one draw needn't show every extreme that they name: `antenna_row_lookup`: each antenna appears once. `chan_order`: each frequency index appears once.
All inputs are finite; a program needn't handle non-finite values.
Results may differ from a plain program's by a relative error of at most 0.004.
Values may be sent and summed in bfloat16 or wider, within the bound.
A program may use at most 64 MiB of HBM per device.

v0:
```python
import math
import jax
import jax.numpy as jnp
from jax import lax
from jax.sharding import PartitionSpec as P

INTEG = 8


def partner_2(value, axis, distance):
    mask = 2**distance
    pairs = [(source, source ^ mask) for source in range(lax.axis_size(axis))]
    return lax.ppermute(value, axis, pairs)


def roll_rows(state, shifts):
    length = state.shape[1]
    doubled = jnp.concatenate([state, state], axis=1)

    def one_row(row, shift):
        return lax.dynamic_slice_in_dim(row, length - shift, length, 0)

    return jax.vmap(one_row)(doubled, shifts)


def pair_round(state, shifts, stride):
    count, length, width = state.shape
    grouped = state.reshape(count // (2 * stride), 2, stride, length, width)
    lower = jnp.broadcast_to(grouped[:, 0:1], grouped.shape).reshape(state.shape)
    upper = jnp.broadcast_to(grouped[:, 1:2], grouped.shape).reshape(state.shape)
    return lower + roll_rows(upper, shifts)


def partner_round(state, partner, upper_side, shifts):
    lower = jnp.where(upper_side, partner, state)
    upper = jnp.where(upper_side, state, partner)
    return lower + roll_rows(upper, shifts)


def beam_weights(gain_pair, freq, pos_rows, dirs):
    geometry = pos_rows[0][:, None] * dirs[0][None, :]
    geometry = geometry + pos_rows[1][:, None] * dirs[1][None, :]
    geometry = geometry + pos_rows[2][:, None] * dirs[2][None, :]
    phase = (2.0 * math.pi * freq)[:, None, None] * geometry[None]
    cosine = jnp.cos(phase)
    sine = jnp.sin(phase)
    g_re = gain_pair[0][:, :, None]
    g_im = gain_pair[1][:, :, None]
    factor = 1.0 / math.sqrt(pos_rows.shape[1])
    w_re = ((g_re * cosine + g_im * sine) * factor).astype(jnp.bfloat16)
    w_im = ((g_im * cosine - g_re * sine) * factor).astype(jnp.bfloat16)
    upper_rows = jnp.concatenate([w_re, w_im], axis=2)
    lower_rows = jnp.concatenate([-w_im, w_re], axis=2)
    return jnp.stack([upper_rows, lower_rows], axis=1)


def integrate(power, chans):
    count, samples, width = power.shape
    binned = jnp.mean(power.reshape(count, samples // INTEG, INTEG, width), axis=2)
    centred = binned - jnp.mean(binned, axis=1, keepdims=True)
    return centred * (1.0 / math.sqrt(chans))


def shards(voltages, gains, positions, directions, antenna_row_lookup, chan_order, delays):
    chan_count = lax.axis_size("chan")
    band_count = lax.axis_size("band")
    per_dev = gains.shape[2]
    in_band = per_dev * chan_count
    total = in_band * band_count
    chan_index = lax.axis_index("chan")
    band_index = lax.axis_index("band")
    base = band_index * in_band + chan_index * per_dev
    freq = 1.0 + lax.dynamic_slice_in_dim(chan_order, base, per_dev).astype(jnp.float32) / total
    pos_rows = positions[:, antenna_row_lookup]
    weights = beam_weights(gains[:, 0], freq, pos_rows, directions)
    turned = lax.all_to_all(voltages, "chan", split_axis=3, concat_axis=1, tiled=True)
    flat = turned.reshape(turned.shape[0], turned.shape[1], turned.shape[3], turned.shape[4])
    beams = jnp.einsum("pacn,cpaq->cnq", flat, weights, preferred_element_type=jnp.float32)
    half = beams.shape[2] // 2
    power = beams[:, :, :half] * beams[:, :, :half] + beams[:, :, half:] * beams[:, :, half:]
    state = integrate(power, total)
    flat_delays = delays.reshape(delays.shape[0], total)
    local_bits = per_dev.bit_length() - 1
    chan_bits = chan_count.bit_length() - 1
    band_bits = band_count.bit_length() - 1
    bit = 0
    shifts = lax.dynamic_slice_in_dim(flat_delays[bit], base, per_dev)
    state = pair_round(state, shifts, 1 << bit)
    for bit in range(chan_bits):
        level_no = local_bits + bit
        shifts = lax.dynamic_slice_in_dim(flat_delays[level_no], base, per_dev)
        partner = partner_2(state, "chan", bit)
        upper_side = chan_index // (1 << bit) % 2 == 1
        state = partner_round(state, partner, upper_side, shifts)
    for bit in range(band_bits):
        level_no = local_bits + chan_bits + bit
        shifts = lax.dynamic_slice_in_dim(flat_delays[level_no], base, per_dev)
        partner = partner_2(state, "band", bit)
        upper_side = band_index // (1 << bit) % 2 == 1
        state = partner_round(state, partner, upper_side, shifts)
    return state.reshape(1, per_dev, state.shape[1], state.shape[2])


def solution(mesh):
    placed = (
        P(None, "chan", "band", None, "group"),
        P(None, "band", "chan", None),
        P(),
        P(None, ("group", "beam")),
        P(),
        P(),
        P(),
    )
    return jax.shard_map(
        shards,
        mesh=mesh,
        in_specs=placed,
        out_specs=P("band", "chan", None, ("group", "beam")),
        check_vma=False,
    )
```

profile of v0, /device:TPU:0, one launch (start us, length us, event | category | flops | bytes accessed | tf_op | source)
XLA Modules:
  0.0 94.2 jit_solution(8014257760844754673)
XLA Ops:
  0.0 3.5 %copy.29 = bf16[2,256,1,8,256]{4,1,2,0,3:T(8,128)(2,1)} copy(bf16[2,256,1,8,256]{4,3,2,1,0:T(8,128)(2,1)} %param.7) | data formatting | bytes 4194304 | tf_op args[0]
  3.5 6.4 %all-to-all-start = ((bf16[2,256,1,8,256]{4,1,2,0,3:T(8,128)(2,1)}), bf16[2,256,1,8,256]{4,1,2,0,3:T(8,128)(2,1)S(1)}, u32[]{:S(2)}, u32[]{:S(2)}) async-start(bf16[2,256,1,8,256]{4,1,2,0,3:T(8,128)(2,1)} %copy.29), calls=%async_computation | async-start | bytes 4194304 | tf_op jit(solution)/shard_map/all_to_all | solution.py:76
  9.9 0.2 copy.27
  10.3 2.8 %gather_fusion = f32[1024,3]{1,0:T(8,128)S(1)} fusion(f32[3,1024]{0,1:T(8,128)S(1)} %copy.27, s32[1024]{0:T(1024)S(1)} %fusion.21), kind=kCustom, calls=%fused_computation | custom fusion | bytes 28672 | tf_op jit(solution)/shard_map/gather | solution.py:74
  13.3 0.8 slice_reduce_fusion.2
  14.1 0.5 multiply_add_fusion
  14.6 15.9 %fusion.10 = bf16[2,1024,512]{2,1,0:T(8,128)(2,1)S(1)} fusion(f32[2,1024]{1,0:T(2,128)S(1)} %get-tuple-element.15, f32[1024,512]{1,0:T(8,128)S(1)} %multiply_add_fusion, f32[2]{0:T(128)S(1)} %add_multiply_fusion, f32[2,1024]{1,0:T(2,128)S(1)} %get-tuple-element.14), kind=kLoop, calls=%fused_computation.17 | loop fusion | flops 6291456 | bytes 4210696 | tf_op jit(solution)/shard_map/convert_element_type | solution.py:50
  30.4 16.1 %fusion.31 = (bf16[2,1024,512]{2,1,0:T(8,128)(2,1)S(1)}, bf16[2,1024,512]{2,1,0:T(8,128)(2,1)S(1)}) fusion(f32[2,1024]{1,0:T(2,128)S(1)} %get-tuple-element.14, f32[1024,512]{1,0:T(8,128)S(1)} %multiply_add_fusion, f32[2]{0:T(128)S(1)} %add_multiply_fusion, f32[2,1024]{1,0:T(2,128)S(1)} %get-tuple-element.15), kind=kLoop, calls=%fused_computation.73 | loop fusion | flops 9437184 | bytes 6307848 | tf_op jit(solution)/shard_map/neg | solution.py:53
  46.6 3.9 %maximum_bitcast_fusion = (bf16[2,1,1024,1024]{3,2,1,0:T(8,128)(2,1)}, bf16[2,1,1024,1024]{3,2,1,0:T(8,128)(2,1)}) fusion(bf16[2,1024,512]{2,1,0:T(8,128)(2,1)S(1)} %get-tuple-element.9, bf16[2,1024,512]{2,1,0:T(8,128)(2,1)S(1)} %fusion.10, bf16[2,1024,512]{2,1,0:T(8,128)(2,1)S(1)} %get-tuple-element.8), kind=kLoop, calls=%fused_computation.21 | loop fusion | flops 16777216 | bytes 14680064 | tf_op jit(solution)/shard_map/stack | solution.py:54
  50.5 7.7 %all-to-all-done = bf16[2,256,1,8,256]{4,1,2,0,3:T(8,128)(2,1)S(1)} async-done(((bf16[2,256,1,8,256]{4,1,2,0,3:T(8,128)(2,1)}), bf16[2,256,1,8,256]{4,1,2,0,3:T(8,128)(2,1)S(1)}, u32[]{:S(2)}, u32[]{:S(2)}) %all-to-all-start) | async-done | bytes 2097184 | tf_op jit(solution)/shard_map/all_to_all | solution.py:76
  58.1 1.5 %copy.30 = bf16[2,256,1,8,256]{4,1,3,0,2:T(8,128)(2,1)} copy(bf16[2,256,1,8,256]{4,1,2,0,3:T(8,128)(2,1)S(1)} %all-to-all-done) | data formatting | bytes 4194304 | tf_op jit(solution)/shard_map/all_to_all | solution.py:76
  59.6 3.1 %copy.31 = bf16[2,4,256,1,2,256]{2,1,5,0,4,3:T(4,128)(2,1)S(1)} copy(bf16[2,4,256,1,2,256]{5,2,4,1,0,3:T(8,128)(2,1)} %bitcast.73) | data formatting | bytes 4194304 | tf_op jit(solution)/shard_map/all_to_all | solution.py:76
  62.7 2.7 %reshape.148 = bf16[2,1024,2,256]{1,3,0,2:T(8,128)(2,1)} reshape(bf16[2,4,256,1,2,256]{2,1,5,0,4,3:T(4,128)(2,1)S(1)} %copy.31) | data formatting | bytes 4194304 | tf_op jit(solution)/shard_map/reshape | solution.py:77
  65.4 5.4 %fusion.14 = f32[2,256,1024]{2,1,0:T(8,128)S(1)} fusion(bf16[2,1024,2,256]{1,3,0,2:T(8,128)(2,1)} %reshape.148, bf16[2,1,1024,1024]{3,2,1,0:T(8,128)(2,1)} %get-tuple-element.11, bf16[2,1,1024,1024]{3,2,1,0:T(8,128)(2,1)} %get-tuple-element.10), kind=kOutput, calls=%fused_computation.24 | convolution fusion | flops 2164260864 | bytes 12582912 | tf_op jit(solution)/shard_map/pacn,cpaq->cnq/dot_general | solution.py:78
  70.9 0.5 fusion.19
  71.6 1.1 %gather_fusion.1 = f32[2,32,512]{2,0,1:T(2,128)S(1)} fusion(f32[2,64,512]{2,0,1:T(2,128)S(1)} %pad_maximum_fusion, s32[2]{0:T(128)S(1)} %fusion.29), kind=kCustom, calls=%fused_computation.1 | custom fusion | bytes 262168 | tf_op jit(solution)/shard_map/vmap()/gather | solution.py:21
  73.0 4.8 %collective-permute-done = f32[2,32,512]{2,0,1:T(2,128)S(1)} collective-permute-done((f32[2,32,512]{2,0,1:T(2,128)S(1)}, f32[2,32,512]{2,0,1:T(2,128)S(1)}, u32[]{:S(2)}, u32[]{:S(2)}) %collective-permute-start) | collective-permute-done | bytes 131104 | tf_op jit(solution)/shard_map/ppermute | solution.py:13
  78.0 1.1 %gather_fusion.2 = f32[2,32,512]{2,0,1:T(2,128)S(1)} fusion(f32[2,64,512]{2,0,1:T(2,128)S(1)} %pad_maximum_fusion.1, s32[2]{0:T(128)S(1)} %fusion.28), kind=kCustom, calls=%fused_computation.2 | custom fusion | bytes 262168 | tf_op jit(solution)/shard_map/vmap()/gather | solution.py:21
  79.5 6.5 %collective-permute-done.1 = f32[2,32,512]{2,0,1:T(2,128)S(1)} collective-permute-done((f32[2,32,512]{2,0,1:T(2,128)S(1)}, f32[2,32,512]{2,0,1:T(2,128)S(1)}, u32[]{:S(2)}, u32[]{:S(2)}) %collective-permute-start.1) | collective-permute-done | bytes 131104 | tf_op jit(solution)/shard_map/ppermute | solution.py:13
  86.1 1.1 %gather_fusion.3 = f32[2,32,512]{2,0,1:T(2,128)S(1)} fusion(f32[2,64,512]{2,0,1:T(2,128)S(1)} %pad_maximum_fusion.2, s32[2]{0:T(128)S(1)} %fusion.27), kind=kCustom, calls=%fused_computation.3 | custom fusion | bytes 262168 | tf_op jit(solution)/shard_map/vmap()/gather | solution.py:21
  87.2 1.6 %collective-permute-start.2 = (f32[2,32,512]{2,0,1:T(2,128)S(1)}, f32[2,32,512]{2,0,1:T(2,128)S(1)}, u32[]{:S(2)}, u32[]{:S(2)}) collective-permute-start(f32[2,32,512]{2,0,1:T(2,128)S(1)} %bitcast.75), channel_id=1, source_target_pairs={{0,2},{2,0},{1,3},{3,1},{4,6},{6,4},{5,7},{7,5},{8,10},{10,8},{9,1... | collective-permute-start | bytes 393224 | tf_op jit(solution)/shard_map/ppermute | solution.py:13
  88.9 3.3 %collective-permute-done.2 = f32[2,32,512]{2,0,1:T(2,128)S(1)} collective-permute-done((f32[2,32,512]{2,0,1:T(2,128)S(1)}, f32[2,32,512]{2,0,1:T(2,128)S(1)}, u32[]{:S(2)}, u32[]{:S(2)}) %collective-permute-start.2) | collective-permute-done | bytes 131104 | tf_op jit(solution)/shard_map/ppermute | solution.py:13
  92.4 1.1 %gather_fusion.4 = f32[2,32,512]{2,0,1:T(2,128)S(1)} fusion(f32[2,64,512]{2,0,1:T(2,128)S(1)} %pad_maximum_fusion.3, s32[2]{0:T(128)S(1)} %fusion.26), kind=kCustom, calls=%fused_computation.4 | custom fusion | bytes 262168 | tf_op jit(solution)/shard_map/vmap()/gather | solution.py:21
  93.5 0.7 copy.32
  (43 shorter events, 1.8 us)
Async XLA Ops:
  0.0 9.9 %copy-start = (f32[3,1024]{1,0:T(4,128)S(1)}, f32[3,1024]{1,0:T(4,128)}, u32[]{:S(2)}) copy-start(f32[3,1024]{1,0:T(4,128)} %param.9) | copy-start | bytes 36868
  0.0 10.2 %copy-start.3 = (s32[4,2,8]{2,1,0:T(2,128)S(1)}, s32[4,2,8]{2,1,0:T(2,128)}, u32[]{:S(2)}) copy-start(s32[4,2,8]{2,1,0:T(2,128)} %param.13) | copy-start | bytes 772
  0.0 10.3 %copy-start.4 = (s32[1024]{0:T(1024)S(1)}, s32[1024]{0:T(1024)}, u32[]{:S(2)}) copy-start(s32[1024]{0:T(1024)} %param.11) | copy-start | bytes 12292
  0.0 13.1 %copy-start.5 = (s32[16]{0:T(128)S(1)}, s32[16]{0:T(128)}, u32[]{:S(2)}) copy-start(s32[16]{0:T(128)} %param.12) | copy-start | bytes 196
  3.5 10.6 %copy-start.2 = (f32[3,512]{1,0:T(4,128)S(1)}, f32[3,512]{1,0:T(4,128)}, u32[]{:S(2)}) copy-start(f32[3,512]{1,0:T(4,128)} %param.10) | copy-start | bytes 18436
  3.5 10.6 %copy-start.1 = (f32[2,1,2,1024]{3,2,1,0:T(2,128)S(1)}, f32[2,1,2,1024]{3,2,1,0:T(2,128)}, u32[]{:S(2)}) copy-start(f32[2,1,2,1024]{3,2,1,0:T(2,128)} %param.8) | copy-start | bytes 49156
  3.5 54.6 %all-to-all-start = ((bf16[2,256,1,8,256]{4,1,2,0,3:T(8,128)(2,1)}), bf16[2,256,1,8,256]{4,1,2,0,3:T(8,128)(2,1)S(1)}, u32[]{:S(2)}, u32[]{:S(2)}) async-start(bf16[2,256,1,8,256]{4,1,2,0,3:T(8,128)(2,1)} %copy.29), calls=%async_computation | async-start | bytes 4194304 | tf_op jit(solution)/shard_map/all_to_all | solution.py:76
  72.8 5.0 %collective-permute-start = (f32[2,32,512]{2,0,1:T(2,128)S(1)}, f32[2,32,512]{2,0,1:T(2,128)S(1)}, u32[]{:S(2)}, u32[]{:S(2)}) collective-permute-start(f32[2,32,512]{2,0,1:T(2,128)S(1)} %broadcast_add_fusion), channel_id=1, source_target_pairs={{0,4},{4,0},{8,12},{12,8},{1,5},{5,1},{9,13},{13,9},{2,6},{6,2},{1... | collective-permute-start | bytes 393224 | tf_op jit(solution)/shard_map/ppermute | solution.py:13
  79.2 6.8 %collective-permute-start.1 = (f32[2,32,512]{2,0,1:T(2,128)S(1)}, f32[2,32,512]{2,0,1:T(2,128)S(1)}, u32[]{:S(2)}, u32[]{:S(2)}) collective-permute-start(f32[2,32,512]{2,0,1:T(2,128)S(1)} %select_add_fusion.1), channel_id=1, source_target_pairs={{0,8},{4,12},{8,0},{12,4},{1,9},{5,13},{9,1},{13,5},{2,10},{6,14},... | collective-permute-start | bytes 393224 | tf_op jit(solution)/shard_map/ppermute | solution.py:13
  87.2 5.0 %collective-permute-start.2 = (f32[2,32,512]{2,0,1:T(2,128)S(1)}, f32[2,32,512]{2,0,1:T(2,128)S(1)}, u32[]{:S(2)}, u32[]{:S(2)}) collective-permute-start(f32[2,32,512]{2,0,1:T(2,128)S(1)} %bitcast.75), channel_id=1, source_target_pairs={{0,2},{2,0},{1,3},{3,1},{4,6},{6,4},{5,7},{7,5},{8,10},{10,8},{9,1... | collective-permute-start | bytes 393224 | tf_op jit(solution)/shard_map/ppermute | solution.py:13
where the time goes:
time: 94.5 us; the launch traced here: 94.2 us
  other arithmetic  38.1 us (40%)
  waiting for transfers between devices  22.3 us (24%)
  local copies, waits for them, and re-layouts  20 us (21%)
  starting transfers between devices  8.15 us (9%)
  matrix products  5.44 us (6%)
    neg x1, other arithmetic, beam_weights(): lower_rows = jnp.concatenate([-w_im, w_re], axis=2)  16.1 us
    convert_element_type x1, other arithmetic, beam_weights(): w_re = ((g_re * cosine + g_im * sine) * factor).astype(jnp.bfloat16)  15.9 us
    ppermute x3, waiting for transfers between devices, partner_2(): return lax.ppermute(value, axis, pairs)  14.6 us
    all_to_all x1, waiting for transfers between devices, shards(): lax.all_to_all(voltages, 'chan', split_axis=3, concat_axis=1, tiled=True)  7.65 us
    all_to_all x1, starting transfers between devices, shards(): lax.all_to_all(voltages, 'chan', split_axis=3, concat_axis=1, tiled=True)  6.45 us
    dot_general x1, matrix products, shards(): jnp.einsum('pacn,cpaq->cnq', flat, weights, preferred_element_type=jnp.fl...  5.44 us
    all_to_all x2, local copies, waits for them, and re-layouts, shards(): lax.all_to_all(voltages, 'chan', split_axis=3, concat_axis=1, tiled=True)  4.56 us
    gather x4, local copies, waits for them, and re-layouts, one_row(): return lax.dynamic_slice_in_dim(row, length - shift, length, 0)  4.3 us
  transfers between devices with their start and end apart: 4, of which 4 were waited for; matrix products, arithmetic and copies ran while one was open for 43% of the time, Pallas kernels for 0%

commit v1 on v0

--- a/solution.py
+++ b/solution.py
@@ -73,7 +73,10 @@
     freq = 1.0 + lax.dynamic_slice_in_dim(chan_order, base, per_dev).astype(jnp.float32) / total
     pos_rows = positions[:, antenna_row_lookup]
     weights = beam_weights(gains[:, 0], freq, pos_rows, directions)
-    turned = lax.all_to_all(voltages, "chan", split_axis=3, concat_axis=1, tiled=True)
+    n_dev = lax.axis_size("chan")
+    shards_2 = jnp.stack(jnp.split(voltages, n_dev, axis=3), axis=0)
+    shards_2 = lax.all_to_all(shards_2, "chan", split_axis=0, concat_axis=0)
+    turned = jnp.concatenate(shards_2, axis=1)
     flat = turned.reshape(turned.shape[0], turned.shape[1], turned.shape[3], turned.shape[4])
     beams = jnp.einsum("pacn,cpaq->cnq", flat, weights, preferred_element_type=jnp.float32)
     half = beams.shape[2] // 2

time: 94.5 us -> 102 us (1.079)
  other arithmetic: 38.1 us -> 42.8 us
  local copies, waits for them, and re-layouts: 20 us -> 23.6 us
    another operation x0 -> x3, local copies, waits for them, and re-layouts: none -> 9.6 us  [the longest x2 6.37 us: shards(): shards_2 = jnp.stack(jnp.split(voltages, n_dev, axis=3), axis=0)]
    another operation x0 -> x1, other arithmetic: none -> 4.69 us  [shards(): shards_2 = jnp.stack(jnp.split(voltages, n_dev, axis=3), axis=0)]
    all_to_all x2 -> x0, local copies, waits for them, and re-layouts: 4.56 us -> none  [shards(): lax.all_to_all(voltages, 'chan', split_axis=3, concat_axis=1, tiled=True)]
    unnamed x14 -> x13, local copies, waits for them, and re-layouts: 3.71 us -> 0.25 us
    reshape x1, local copies, waits for them, and re-layouts: 2.74 us -> 4.82 us  [shards(): turned = jnp.concatenate(shards_2, axis=1)]
  transfers between devices with their start and end apart: 4 -> 4, of which waited for: 4 -> 4; matrix products, arithmetic and copies ran while one was open for 43% -> 40% of each run, Pallas kernels for 0% -> 0%
where the time goes in v1:
time: 102 us
  other arithmetic  42.8 us (42%)
  local copies, waits for them, and re-layouts  23.6 us (23%)
  waiting for transfers between devices  22.3 us (22%)
  starting transfers between devices  8.15 us (8%)
  matrix products  4.76 us (5%)
    neg x1, other arithmetic, beam_weights(): lower_rows = jnp.concatenate([-w_im, w_re], axis=2)  16.1 us
    convert_element_type x1, other arithmetic, beam_weights(): w_re = ((g_re * cosine + g_im * sine) * factor).astype(jnp.bfloat16)  15.9 us
    ppermute x3, waiting for transfers between devices, partner_2(): return lax.ppermute(value, axis, pairs)  14.6 us
    all_to_all x1, waiting for transfers between devices, shards(): shards_2 = lax.all_to_all(shards_2, 'chan', split_axis=0, concat_axis=0)  7.65 us
    all_to_all x1, starting transfers between devices, shards(): shards_2 = lax.all_to_all(shards_2, 'chan', split_axis=0, concat_axis=0)  6.45 us
    another operation x2, local copies, waits for them, and re-layouts, shards(): shards_2 = jnp.stack(jnp.split(voltages, n_dev, axis=3), axis=0)  6.37 us
    reshape x1, local copies, waits for them, and re-layouts, shards(): turned = jnp.concatenate(shards_2, axis=1)  4.82 us
    dot_general x1, matrix products, shards(): jnp.einsum('pacn,cpaq->cnq', flat, weights, preferred_element_type=jnp.fl...  4.76 us
  transfers between devices with their start and end apart: 4, of which 4 were waited for; matrix products, arithmetic and copies ran while one was open for 40% of the time, Pallas kernels for 0%

profile of v1, /device:TPU:0, one launch (start us, length us, event | category | flops | bytes accessed | tf_op | source)
XLA Modules:
  0.0 101.9 jit_solution(6555362902644605171)
XLA Ops:
  0.0 2.1 %slice_bitcast_fusion.3 = bf16[1,2,256,1,2,256]{5,4,2,1,3,0:T(2,128)(2,1)S(1)} fusion(bf16[2,256,1,8,256]{4,3,2,1,0:T(8,128)(2,1)} %param.7), kind=kLoop, calls=%fused_computation.37 | loop fusion | bytes 1048576 | tf_op jit(solution)/shard_map/stack | solution.py:77
  2.1 4.2 %slice_bitcast_fusion.2 = (bf16[1,2,256,1,2,256]{5,4,2,1,3,0:T(2,128)(2,1)S(1)}, bf16[1,2,256,1,2,256]{5,4,2,1,3,0:T(2,128)(2,1)S(1)}, bf16[1,2,256,1,2,256]{5,4,2,1,3,0:T(2,128)(2,1)S(1)}) fusion(bf16[2,256,1,8,256]{4,3,1,0,2:T(8,128)(2,1)} %bitcast.82), kind=kLoop, calls=%fused_computation.36 | loop fusion | bytes 3145728 | tf_op jit(solution)/shard_map/stack | solution.py:77
  6.4 4.7 %pad_maximum_fusion = bf16[4,2,256,1,2,256]{5,4,2,1,3,0:T(2,128)(2,1)} fusion(bf16[1,2,256,1,2,256]{5,4,2,1,3,0:T(2,128)(2,1)S(1)} %get-tuple-element.13, bf16[1,2,256,1,2,256]{5,4,2,1,3,0:T(2,128)(2,1)S(1)} %get-tuple-element.14, bf16[1,2,256,1,2,256]{5,4,2,1,3,0:T(2,128)(2,1)S(1)} %slice_bitcast_fusion.3, ...), kind=kLoop, calls=%fused_computation.23 | loop fusion | flops 3145728 | bytes 4194304 | tf_op jit(solution)/shard_map/stack | solution.py:77
  11.1 6.5 %all-to-all-start = ((bf16[4,2,256,1,2,256]{5,4,2,1,3,0:T(2,128)(2,1)}), bf16[4,2,256,1,2,256]{5,4,2,1,3,0:T(2,128)(2,1)S(1)}, u32[]{:S(2)}, u32[]{:S(2)}) async-start(bf16[4,2,256,1,2,256]{5,4,2,1,3,0:T(2,128)(2,1)} %pad_maximum_fusion), calls=%async_computation | async-start | bytes 4194304 | tf_op jit(solution)/shard_map/all_to_all | solution.py:78
  17.9 2.8 %gather_fusion = f32[1024,3]{1,0:T(8,128)S(1)} fusion(f32[3,1024]{0,1:T(8,128)S(1)} %copy.19, s32[1024]{0:T(1024)S(1)} %fusion.21), kind=kCustom, calls=%fused_computation | custom fusion | bytes 28672 | tf_op jit(solution)/shard_map/gather | solution.py:74
  20.9 0.8 slice_reduce_fusion.2
  21.7 0.5 multiply_add_fusion
  22.2 15.9 %fusion.10 = bf16[2,1024,512]{2,1,0:T(8,128)(2,1)S(1)} fusion(f32[2,1024]{1,0:T(2,128)S(1)} %get-tuple-element.18, f32[1024,512]{1,0:T(8,128)S(1)} %multiply_add_fusion, f32[2]{0:T(128)S(1)} %add_multiply_fusion, f32[2,1024]{1,0:T(2,128)S(1)} %get-tuple-element.17), kind=kLoop, calls=%fused_computation.17 | loop fusion | flops 6291456 | bytes 4210696 | tf_op jit(solution)/shard_map/convert_element_type | solution.py:50
  38.1 16.1 %fusion.31 = (bf16[2,1024,512]{2,1,0:T(8,128)(2,1)S(1)}, bf16[2,1024,512]{2,1,0:T(8,128)(2,1)S(1)}) fusion(f32[2,1024]{1,0:T(2,128)S(1)} %get-tuple-element.17, f32[1024,512]{1,0:T(8,128)S(1)} %multiply_add_fusion, f32[2]{0:T(128)S(1)} %add_multiply_fusion, f32[2,1024]{1,0:T(2,128)S(1)} %get-tuple-element.18), kind=kLoop, calls=%fused_computation.78 | loop fusion | flops 9437184 | bytes 6307848 | tf_op jit(solution)/shard_map/neg | solution.py:53
  54.2 3.9 %maximum_bitcast_fusion = (bf16[2,1,1024,1024]{3,2,1,0:T(8,128)(2,1)}, bf16[2,1,1024,1024]{3,2,1,0:T(8,128)(2,1)}) fusion(bf16[2,1024,512]{2,1,0:T(8,128)(2,1)S(1)} %get-tuple-element.9, bf16[2,1024,512]{2,1,0:T(8,128)(2,1)S(1)} %fusion.10, bf16[2,1024,512]{2,1,0:T(8,128)(2,1)S(1)} %get-tuple-element.8), kind=kLoop, calls=%fused_computation.21 | loop fusion | flops 16777216 | bytes 14680064 | tf_op jit(solution)/shard_map/stack | solution.py:54
  58.1 7.7 %all-to-all-done = bf16[4,2,256,1,2,256]{5,4,2,1,3,0:T(2,128)(2,1)S(1)} async-done(((bf16[4,2,256,1,2,256]{5,4,2,1,3,0:T(2,128)(2,1)}), bf16[4,2,256,1,2,256]{5,4,2,1,3,0:T(2,128)(2,1)S(1)}, u32[]{:S(2)}, u32[]{:S(2)}) %all-to-all-start) | async-done | bytes 2097184 | tf_op jit(solution)/shard_map/all_to_all | solution.py:78
  65.8 4.8 %copy.18 = bf16[2,4,256,1,2,256]{2,1,5,0,4,3:T(4,128)(2,1)} copy(bf16[2,4,256,1,2,256]{5,4,2,0,3,1:T(2,128)(2,1)S(1)} %bitcast.80) | data formatting | bytes 4194304 | tf_op jit(solution)/shard_map/reshape | solution.py:79
  70.6 3.2 %reshape_reshape.3 = bf16[2,1024,2,256]{1,3,0,2:T(8,128)(2,1)S(1)} reshape(bf16[2,4,256,1,2,256]{2,1,5,0,4,3:T(4,128)(2,1)} %copy.18) | data formatting | bytes 4194304 | tf_op jit(solution)/shard_map/reshape;reshape | solution.py:80
  73.8 4.8 %fusion.14 = f32[2,256,1024]{2,1,0:T(8,128)S(1)} fusion(bf16[2,1024,2,256]{1,3,0,2:T(8,128)(2,1)S(1)} %reshape_reshape.3, bf16[2,1,1024,1024]{3,2,1,0:T(8,128)(2,1)} %get-tuple-element.11, bf16[2,1,1024,1024]{3,2,1,0:T(8,128)(2,1)} %get-tuple-element.10), kind=kOutput, calls=%fused_computation.25 | convolution fusion | flops 2151677952 | bytes 12582912 | tf_op jit(solution)/shard_map/pacn,cpaq->cnq/dot_general | solution.py:81
  78.6 0.5 fusion.19
  79.3 1.1 %gather_fusion.1 = f32[2,32,512]{2,0,1:T(2,128)S(1)} fusion(f32[2,64,512]{2,0,1:T(2,128)S(1)} %pad_maximum_fusion.1, s32[2]{0:T(128)S(1)} %fusion.29), kind=kCustom, calls=%fused_computation.1 | custom fusion | bytes 262168 | tf_op jit(solution)/shard_map/vmap()/gather | solution.py:21
  80.7 4.8 %collective-permute-done = f32[2,32,512]{2,0,1:T(2,128)S(1)} collective-permute-done((f32[2,32,512]{2,0,1:T(2,128)S(1)}, f32[2,32,512]{2,0,1:T(2,128)S(1)}, u32[]{:S(2)}, u32[]{:S(2)}) %collective-permute-start) | collective-permute-done | bytes 131104 | tf_op jit(solution)/shard_map/ppermute | solution.py:13
  85.7 1.1 %gather_fusion.2 = f32[2,32,512]{2,0,1:T(2,128)S(1)} fusion(f32[2,64,512]{2,0,1:T(2,128)S(1)} %pad_maximum_fusion.2, s32[2]{0:T(128)S(1)} %fusion.28), kind=kCustom, calls=%fused_computation.2 | custom fusion | bytes 262168 | tf_op jit(solution)/shard_map/vmap()/gather | solution.py:21
  87.2 6.5 %collective-permute-done.1 = f32[2,32,512]{2,0,1:T(2,128)S(1)} collective-permute-done((f32[2,32,512]{2,0,1:T(2,128)S(1)}, f32[2,32,512]{2,0,1:T(2,128)S(1)}, u32[]{:S(2)}, u32[]{:S(2)}) %collective-permute-start.1) | collective-permute-done | bytes 131104 | tf_op jit(solution)/shard_map/ppermute | solution.py:13
  93.8 1.1 %gather_fusion.3 = f32[2,32,512]{2,0,1:T(2,128)S(1)} fusion(f32[2,64,512]{2,0,1:T(2,128)S(1)} %pad_maximum_fusion.3, s32[2]{0:T(128)S(1)} %fusion.27), kind=kCustom, calls=%fused_computation.3 | custom fusion | bytes 262168 | tf_op jit(solution)/shard_map/vmap()/gather | solution.py:21
  94.9 1.6 %collective-permute-start.2 = (f32[2,32,512]{2,0,1:T(2,128)S(1)}, f32[2,32,512]{2,0,1:T(2,128)S(1)}, u32[]{:S(2)}, u32[]{:S(2)}) collective-permute-start(f32[2,32,512]{2,0,1:T(2,128)S(1)} %bitcast.83), channel_id=1, source_target_pairs={{0,2},{2,0},{1,3},{3,1},{4,6},{6,4},{5,7},{7,5},{8,10},{10,8},{9,1... | collective-permute-start | bytes 393224 | tf_op jit(solution)/shard_map/ppermute | solution.py:13
  96.7 3.3 %collective-permute-done.2 = f32[2,32,512]{2,0,1:T(2,128)S(1)} collective-permute-done((f32[2,32,512]{2,0,1:T(2,128)S(1)}, f32[2,32,512]{2,0,1:T(2,128)S(1)}, u32[]{:S(2)}, u32[]{:S(2)}) %collective-permute-start.2) | collective-permute-done | bytes 131104 | tf_op jit(solution)/shard_map/ppermute | solution.py:13
  100.1 1.1 %gather_fusion.4 = f32[2,32,512]{2,0,1:T(2,128)S(1)} fusion(f32[2,64,512]{2,0,1:T(2,128)S(1)} %pad_maximum_fusion.4, s32[2]{0:T(128)S(1)} %fusion.26), kind=kCustom, calls=%fused_computation.4 | custom fusion | bytes 262168 | tf_op jit(solution)/shard_map/vmap()/gather | solution.py:21
  101.3 0.7 copy.21
  (44 shorter events, 2.0 us)
Async XLA Ops:
  6.4 11.2 %copy-start = (f32[3,1024]{1,0:T(4,128)S(1)}, f32[3,1024]{1,0:T(4,128)}, u32[]{:S(2)}) copy-start(f32[3,1024]{1,0:T(4,128)} %param.9) | copy-start | bytes 36868
  6.4 11.4 %copy-start.3 = (s32[4,2,8]{2,1,0:T(2,128)S(1)}, s32[4,2,8]{2,1,0:T(2,128)}, u32[]{:S(2)}) copy-start(s32[4,2,8]{2,1,0:T(2,128)} %param.13) | copy-start | bytes 772
  6.4 11.5 %copy-start.4 = (s32[1024]{0:T(1024)S(1)}, s32[1024]{0:T(1024)}, u32[]{:S(2)}) copy-start(s32[1024]{0:T(1024)} %param.11) | copy-start | bytes 12292
  6.4 14.3 %copy-start.5 = (s32[16]{0:T(128)S(1)}, s32[16]{0:T(128)}, u32[]{:S(2)}) copy-start(s32[16]{0:T(128)} %param.12) | copy-start | bytes 196
  11.1 10.6 %copy-start.2 = (f32[3,512]{1,0:T(4,128)S(1)}, f32[3,512]{1,0:T(4,128)}, u32[]{:S(2)}) copy-start(f32[3,512]{1,0:T(4,128)} %param.10) | copy-start | bytes 18436
  11.1 10.6 %copy-start.1 = (f32[2,1,2,1024]{3,2,1,0:T(2,128)S(1)}, f32[2,1,2,1024]{3,2,1,0:T(2,128)}, u32[]{:S(2)}) copy-start(f32[2,1,2,1024]{3,2,1,0:T(2,128)} %param.8) | copy-start | bytes 49156
  11.1 54.6 %all-to-all-start = ((bf16[4,2,256,1,2,256]{5,4,2,1,3,0:T(2,128)(2,1)}), bf16[4,2,256,1,2,256]{5,4,2,1,3,0:T(2,128)(2,1)S(1)}, u32[]{:S(2)}, u32[]{:S(2)}) async-start(bf16[4,2,256,1,2,256]{5,4,2,1,3,0:T(2,128)(2,1)} %pad_maximum_fusion), calls=%async_computation | async-start | bytes 4194304 | tf_op jit(solution)/shard_map/all_to_all | solution.py:78
  80.5 5.0 %collective-permute-start = (f32[2,32,512]{2,0,1:T(2,128)S(1)}, f32[2,32,512]{2,0,1:T(2,128)S(1)}, u32[]{:S(2)}, u32[]{:S(2)}) collective-permute-start(f32[2,32,512]{2,0,1:T(2,128)S(1)} %broadcast_add_fusion), channel_id=1, source_target_pairs={{0,4},{4,0},{8,12},{12,8},{1,5},{5,1},{9,13},{13,9},{2,6},{6,2},{1... | collective-permute-start | bytes 393224 | tf_op jit(solution)/shard_map/ppermute | solution.py:13
  86.9 6.8 %collective-permute-start.1 = (f32[2,32,512]{2,0,1:T(2,128)S(1)}, f32[2,32,512]{2,0,1:T(2,128)S(1)}, u32[]{:S(2)}, u32[]{:S(2)}) collective-permute-start(f32[2,32,512]{2,0,1:T(2,128)S(1)} %select_add_fusion.1), channel_id=1, source_target_pairs={{0,8},{4,12},{8,0},{12,4},{1,9},{5,13},{9,1},{13,5},{2,10},{6,14},... | collective-permute-start | bytes 393224 | tf_op jit(solution)/shard_map/ppermute | solution.py:13
  94.9 5.0 %collective-permute-start.2 = (f32[2,32,512]{2,0,1:T(2,128)S(1)}, f32[2,32,512]{2,0,1:T(2,128)S(1)}, u32[]{:S(2)}, u32[]{:S(2)}) collective-permute-start(f32[2,32,512]{2,0,1:T(2,128)S(1)} %bitcast.83), channel_id=1, source_target_pairs={{0,2},{2,0},{1,3},{3,1},{4,6},{6,4},{5,7},{7,5},{8,10},{10,8},{9,1... | collective-permute-start | bytes 393224 | tf_op jit(solution)/shard_map/ppermute | solution.py:13
